TPU v7x, 32 devices: a whole 2x2x4 slice. The times are simulated.
32 devices in a mesh: blk: 8 (over z, y), rep: 4 (over x, core).
Axes of the slice: x: 2, y: 2, z: 4, core: 2. Of those that a mesh axis runs over, the one named last changes fastest.
Arguments:
- point_xyz: float32 [3, 16384], P(None, ('blk', 'rep')), may hold values from -6 to 6
- point_attrs: float32 [5, 16384], P(None, ('blk', 'rep')), may hold values from -6 to 6
- scan_yaw: float32 [32], P(('blk', 'rep')), may hold values from -3.140625 to 3.140625
- scan_jitter: float32 [32, 3], P(('blk', 'rep')), may hold values from -0.5 to 0.5
- slot_counts: int32 [32, 8], P(('blk', 'rep')), may hold values from 0 to 64, as said below
- voxel_ids: int32 [16384], P(('blk', 'rep')), may hold values from 0 to 511
- point_weight: float32 [8, 96], replicated, may hold values from -2 to 2
- point_bias: float32 [96], replicated, may hold values from -3 to 3
- conv_one: bfloat16 [2592, 96], replicated, may hold values from -0.1875 to 0.1875
- conv_two: bfloat16 [2592, 128], replicated, may hold values from -0.1875 to 0.1875
- out_grad: bfloat16 [32, 64, 1024], P('rep', 'blk'), may hold values from -6 to 6
Outputs:
- block_out: bfloat16 [32, 64, 1024], P('rep', 'blk')
- attr_grad: float32 [5, 16384], P(None, ('blk', 'rep'))
- jitter_grad: float32 [32, 3], P(('blk', 'rep'))
- conv_one_grad: float32 [2592, 96], replicated
- conv_two_grad: float32 [2592, 128], replicated
Inputs may be any that keep to these rules, and one draw needn't show every extreme that they name: `slot_counts`: used slots out of 64; in every draw some voxel block receives 64 points from every scan of its slab. `voxel_ids`: voxel (x * 8 + y) * 8 + z inside the destination block; entries of unused slots are ignored.
All inputs are finite; a program needn't handle non-finite values.
Results may differ from a plain program's by a relative error of at most 0.006.
Values may be sent and summed in bfloat16 or wider, within the bound.
No kernel may reach another device: no remote copies, remote signals or barrier semaphores. Data moves between devices by JAX's collectives and lax.ppermute only.
A program may use at most 64 MiB of HBM per device.

v0:
```python
import jax
import jax.numpy as jnp
from jax import lax
from jax.sharding import PartitionSpec as P

SLOT_CAP = 64


def with_halo(cells, sides, width):
    for axis, dim in sides:
        count = lax.axis_size(axis)
        ends = count - 1
        head = lax.slice_in_dim(cells, 0, width, axis=dim)
        tail = lax.slice_in_dim(cells, cells.shape[dim] - width, cells.shape[dim], axis=dim)
        cells = jnp.concatenate(
            [
                lax.ppermute(tail, axis, [(i, (i + 1) % count) for i in range(ends)]),
                cells,
                lax.ppermute(head, axis, [((i + 1) % count, i) for i in range(ends)]),
            ],
            axis=dim,
        )
    return cells


def silu_slope(value):
    sigmoid_v = jax.nn.sigmoid(value)
    return sigmoid_v * (1.0 + value * (1.0 - sigmoid_v))


def point_layer(inputs, point_weight, point_bias):
    return (
        lax.dot_general(
            inputs, point_weight, (((0,), (0,)), ((), ())), precision=lax.Precision.HIGHEST
        )
        + point_bias
    )


def back_layer(grad_pre, point_weight):
    return lax.dot_general(
        point_weight, grad_pre, (((1,), (1,)), ((), ())), precision=lax.Precision.HIGHEST
    )


def with_faces(volume, channels):
    padded = with_halo(volume, (("blk", 1), ("rep", 0)), 1)
    shaped = padded.reshape(padded.shape[0], padded.shape[1], -1, channels)
    return jnp.pad(shaped, ((0, 0), (0, 0), (1, 1), (0, 0)))


def conv_apply(padded, weight, channels_in):
    kernel = weight.reshape(3, 3, 3, channels_in, weight.shape[1])
    result = lax.conv_general_dilated(
        padded[None],
        kernel,
        (1, 1, 1),
        "VALID",
        dimension_numbers=("NDHWC", "DHWIO", "NDHWC"),
        preferred_element_type=jnp.float32,
    )[0]
    return result.reshape(-1, weight.shape[1])


def kernel_grad(padded, partner, edge_len):
    channels_in = padded.shape[-1]
    channels_out = partner.shape[-1]
    source = jnp.transpose(padded, (3, 0, 1, 2))[..., None]
    target = partner.reshape(edge_len, edge_len, edge_len, 1, channels_out)
    result = lax.conv_general_dilated(
        source,
        target,
        (1, 1, 1),
        "VALID",
        dimension_numbers=("NDHWC", "DHWIO", "NDHWC"),
        preferred_element_type=jnp.float32,
    )
    return jnp.transpose(result, (1, 2, 3, 0, 4)).reshape(27 * channels_in, channels_out)


def flipped(weight, channels_in):
    taps = weight.reshape(3, 3, 3, channels_in, -1)[::-1, ::-1, ::-1]
    return jnp.swapaxes(taps, 3, 4).reshape(-1, channels_in)


def shards(
    point_xyz,
    point_attrs,
    scan_yaw,
    scan_jitter,
    slot_counts,
    voxel_ids,
    point_weight,
    point_bias,
    conv_one,
    conv_two,
    out_grad,
):
    owners = lax.axis_size("blk")
    edge_len = out_grad.shape[0]
    voxels = edge_len**3
    width_one = conv_one.shape[1]
    width_two = conv_two.shape[1]
    slot_index = lax.broadcasted_iota(jnp.int32, (owners, SLOT_CAP), 1)
    filled = slot_index < slot_counts[0][:, None]
    vox_sent = jnp.where(filled, voxel_ids.reshape(owners, SLOT_CAP), voxels)
    cos_yaw = jnp.cos(scan_yaw[0])
    sin_yaw = jnp.sin(scan_yaw[0])
    rotated_x = cos_yaw * point_xyz[0] - sin_yaw * point_xyz[1] + scan_jitter[0, 0]
    rotated_y = sin_yaw * point_xyz[0] + cos_yaw * point_xyz[1] + scan_jitter[0, 1]
    rotated_z = point_xyz[2] + scan_jitter[0, 2]
    inputs = jnp.concatenate([jnp.stack([rotated_x, rotated_y, rotated_z]), point_attrs], axis=0)
    pre_act = point_layer(inputs, point_weight, point_bias)
    local_feat = jax.nn.silu(pre_act).astype(jnp.bfloat16).reshape(owners, SLOT_CAP, width_one)
    incoming, vox_rows = (
        lax.all_to_all(local_feat, "blk", split_axis=0, concat_axis=0, tiled=True),
        lax.all_to_all(vox_sent, "blk", split_axis=0, concat_axis=0, tiled=True),
    )
    features = incoming.reshape(-1, width_one)
    vox_flat = vox_rows.reshape(-1)
    counts = jax.ops.segment_sum(jnp.ones_like(vox_flat), vox_flat, voxels + 1)[:voxels]
    divisor = jnp.maximum(counts, 1).astype(jnp.float32)
    totals = jax.ops.segment_sum(features.astype(jnp.float32), vox_flat, voxels + 1)[:voxels]
    pooled = lax.optimization_barrier((totals / divisor[:, None]).astype(jnp.bfloat16))
    occupied = (counts > 0).astype(jnp.float32)[:, None]
    pooled_pad = with_faces(pooled.reshape(edge_len, edge_len, -1), width_one)
    act_one = conv_apply(pooled_pad, conv_one, width_one)
    hidden = (occupied * jax.nn.silu(act_one)).astype(jnp.bfloat16)
    hidden_pad = with_faces(hidden.reshape(edge_len, edge_len, -1), width_one)
    out_two = conv_apply(hidden_pad, conv_two, width_one)
    block_out = (occupied * out_two).astype(jnp.bfloat16).reshape(edge_len, edge_len, -1)
    grad_two = jnp.where(
        occupied > 0, out_grad.reshape(voxels, width_two), jnp.zeros((), jnp.bfloat16)
    )
    grad_two_pad = with_faces(grad_two.reshape(edge_len, edge_len, -1), width_two)
    grad_hidden = conv_apply(grad_two_pad, flipped(conv_two, width_one), width_two)
    part_two = kernel_grad(hidden_pad, grad_two, edge_len)
    grad_act = (occupied * grad_hidden * silu_slope(act_one)).astype(jnp.bfloat16)
    grad_act_pad = with_faces(grad_act.reshape(edge_len, edge_len, -1), width_one)
    grad_pooled = conv_apply(grad_act_pad, flipped(conv_one, width_one), width_one)
    part_one = kernel_grad(pooled_pad, grad_act, edge_len)
    one_total, two_total = lax.psum((part_one, part_two), ("blk", "rep"))
    grad_ext = jnp.concatenate([grad_pooled, jnp.zeros((1, width_one), jnp.float32)], axis=0)
    count_ext = jnp.concatenate([divisor, jnp.ones((1,), jnp.float32)])
    grad_feat = grad_ext[vox_flat] / count_ext[vox_flat][:, None]
    returned = lax.all_to_all(
        grad_feat.reshape(owners, SLOT_CAP, width_one),
        "blk",
        split_axis=0,
        concat_axis=0,
        tiled=True,
    )
    grad_pre = returned.reshape(-1, width_one) * silu_slope(pre_act)
    grad_inputs = back_layer(grad_pre, point_weight)
    attr_grad = grad_inputs[3:]
    jitter_grad = jnp.sum(grad_inputs[:3], axis=1)[None, :]
    return (block_out, attr_grad, jitter_grad, one_total, two_total)


def solution(mesh):
    in_specs = (
        P(None, ("blk", "rep")),
        P(None, ("blk", "rep")),
        P(("blk", "rep")),
        P(("blk", "rep"), None),
        P(("blk", "rep"), None),
        P(("blk", "rep")),
        P(),
        P(),
        P(),
        P(),
        P("rep", "blk", None),
    )
    out_specs = (P("rep", "blk", None), P(None, ("blk", "rep")), P(("blk", "rep"), None), P(), P())
    return jax.shard_map(shards, mesh=mesh, in_specs=in_specs, out_specs=out_specs, check_vma=False)
```

profile of v0, /device:TPU:0, one launch (start us, length us, event | category | flops | bytes accessed | tf_op | source)
XLA Modules:
  0.0 269.6 jit_solution(3016571241570396834)
XLA Ops:
  7.2 0.9 reshape.249
  8.0 1.3 compare_select_fusion
  9.4 7.3 %all-to-all-start = ((s32[8,1,64]{2,1,0:T(1,128)}), s32[8,1,64]{2,1,0:T(1,128)S(1)}, u32[]{:S(2)}, u32[]{:S(2)}) async-start(s32[8,1,64]{2,1,0:T(1,128)} %compare_select_fusion), calls=%async_computation | async-start | bytes 8192 | tf_op jit(solution)/shard_map/all_to_all | solution.py:117
  17.5 1.4 fusion.41
  18.8 2.8 %subtract_add_fusion = (f32[1,512]{1,0:T(1,128)S(1)}, f32[1,512]{1,0:T(1,128)S(1)}, f32[1,512]{1,0:T(1,128)S(1)}) fusion(f32[3,512]{1,0:T(4,128)} %param.11, f32[]{:T(128)} %bitcast.4, f32[]{:T(128)} %bitcast.3, f32[]{:T(128)} %bitcast.2, f32[]{:T(128)} %bitcast.5, f32[]{:T(128)} %bitcast.6), kind=kLoop, calls=%fused_computation.81 | loop fusion | flops 4608 | bytes 12308 | tf_op jit(solution)/shard_map/add | solution.py:109
  21.6 1.8 multiply_convert_fusion.3
  23.4 0.8 copy.39
  24.2 0.3 copy.40
  24.5 6.0 %all-to-all-start.1 = ((bf16[8,64,96]{2,1,0:T(8,128)(2,1)}), bf16[8,64,96]{2,1,0:T(8,128)(2,1)S(1)}, u32[]{:S(2)}, u32[]{:S(2)}) async-start(bf16[8,64,96]{2,1,0:T(8,128)(2,1)} %bitcast.7), calls=%async_computation.1 | async-start | bytes 262144 | tf_op jit(solution)/shard_map/all_to_all | solution.py:116
  30.6 0.5 broadcast.171
  31.1 0.7 reduce.15
  31.9 4.1 %scatter_custom_fusion = s32[513]{0:T(1024)S(1)} fusion(s32[512]{0:T(512)S(1)} %reshape.282, s32[512]{0:T(512)S(1)} %broadcast.146, s32[]{:T(128)} %constant.8.clone.1), kind=kCustom, calls=%fused_computation.82 | custom fusion | flops 512 | bytes 2056 | tf_op jit(solution)/shard_map/scatter-add | solution.py:121
  36.3 0.1 bitcast_select_fusion
  36.5 3.9 %collective-permute-start.8 = (bf16[8,1,1024]{2,1,0:T(2,128)(2,1)S(1)}, bf16[8,1,1024]{2,1,0:T(2,128)(2,1)S(1)}, u32[]{:S(2)}, u32[]{:S(2)}) collective-permute-start(bf16[8,1,1024]{2,1,0:T(2,128)(2,1)S(1)} %get-tuple-element.21), channel_id=1, source_target_pairs={{0,4},{4,8},{8,12},{12,16},{16,20},{20,24},{24,28},{1,5},{5,9},{9,... | collective-permute-start | bytes 49160 | tf_op jit(solution)/shard_map/ppermute | solution.py:17
  40.3 1.3 collective-permute-start.9
  41.7 0.3 collective-permute-done.8
  41.9 4.2 %collective-permute-done.9 = bf16[8,1,1024]{2,1,0:T(2,128)(2,1)S(1)} collective-permute-done((bf16[8,1,1024]{2,1,0:T(2,128)(2,1)S(1)}, bf16[8,1,1024]{2,1,0:T(2,128)(2,1)S(1)}, u32[]{:S(2)}, u32[]{:S(2)}) %collective-permute-start.9) | collective-permute-done | bytes 16416 | tf_op jit(solution)/shard_map/ppermute | solution.py:19
  46.2 1.3 collective-permute-start.10
  47.5 1.3 collective-permute-start.11
  48.8 0.7 copy.38
  49.5 2.3 gather_fusion.1
  51.8 0.7 div.43
  53.0 3.2 %scatter_custom_fusion.1 = f32[513,96]{1,0:T(8,128)S(1)} fusion(s32[512]{0:T(512)S(1)} %reshape.282, bf16[512,96]{1,0:T(8,128)(2,1)S(1)} %bitcast.68, f32[]{:T(128)} %constant.11.clone.1), kind=kCustom, calls=%fused_computation.28 | custom fusion | flops 98304 | bytes 328068 | tf_op jit(solution)/shard_map/scatter-add | solution.py:123
  56.2 0.1 fusion.11
  56.6 3.8 %collective-permute-start = (bf16[8,1,768]{2,1,0:T(2,128)(2,1)S(1)}, bf16[8,1,768]{2,1,0:T(2,128)(2,1)S(1)}, u32[]{:S(2)}, u32[]{:S(2)}) collective-permute-start(bf16[8,1,768]{2,1,0:T(2,128)(2,1)S(1)} %get-tuple-element.27), channel_id=1, source_target_pairs={{0,4},{4,8},{8,12},{12,16},{16,20},{20,24},{24,28},{1,5},{5,9},{9,... | collective-permute-start | bytes 36872 | tf_op jit(solution)/shard_map/ppermute | solution.py:17
  60.4 1.3 collective-permute-start.1
  61.9 4.2 %collective-permute-done.1 = bf16[8,1,768]{2,1,0:T(2,128)(2,1)S(1)} collective-permute-done((bf16[8,1,768]{2,1,0:T(2,128)(2,1)S(1)}, bf16[8,1,768]{2,1,0:T(2,128)(2,1)S(1)}, u32[]{:S(2)}, u32[]{:S(2)}) %collective-permute-start.1) | collective-permute-done | bytes 12320 | tf_op jit(solution)/shard_map/ppermute | solution.py:19
  66.2 3.8 %collective-permute-start.2 = (bf16[1,10,768]{2,1,0:T(8,128)(2,1)S(1)}, bf16[1,10,768]{2,1,0:T(8,128)(2,1)S(1)}, u32[]{:S(2)}, u32[]{:S(2)}) collective-permute-start(bf16[1,10,768]{2,1,0:T(8,128)(2,1)S(1)} %get-tuple-element.19), channel_id=1, source_target_pairs={{0,1},{1,2},{2,3},{4,5},{5,6},{6,7},{8,9},{9,10},{10,11},{12,13},{... | collective-permute-start | bytes 46088 | tf_op jit(solution)/shard_map/ppermute | solution.py:17
  70.0 1.5 collective-permute-start.3
  71.5 0.5 broadcast.172
  72.0 4.0 %fusion.43 = (f32[8,8,8,96]{3,2,1,0:T(8,128)S(1)}, f32[1,8,8,8,96]{4,0,3,2,1:T(1,128)S(1)}) fusion(f32[]{:T(128)} %broadcast.172, bf16[3,3,3,96,128]{4,3,2,1,0:T(8,128)(2,1)S(1)} %bitcast.61, bf16[1,10,10,10,128]{4,3,2,1,0:T(8,128)(2,1)S(1)} %pad_bitcast_fusion.5), kind=kOutput, calls=%fused_computation.94 | convolution fusion | flops 339738624 | bytes 1312772 | tf_op jit(solution)/shard_map/conv_general_dilated | solution.py:54
  76.2 0.3 reshape.252
  76.5 0.1 pad_bitcast_fusion.2
  76.7 4.2 %fusion.42 = (f32[8,8,8,96]{3,2,1,0:T(8,128)S(1)}, f32[1,8,8,8,96]{4,0,3,2,1:T(1,128)S(1)}) fusion(f32[]{:T(128)} %broadcast.172, bf16[3,3,3,96,96]{4,3,2,1,0:T(8,128)(2,1)S(1)} %bitcast.66, bf16[1,10,10,10,96]{4,3,2,1,0:T(8,128)(2,1)S(1)} %get-tuple-element.12), kind=kOutput, calls=%fused_computation.93 | convolution fusion | flops 254803968 | bytes 1082884 | tf_op jit(solution)/shard_map/conv_general_dilated | solution.py:54
  81.1 3.2 %collective-permute-start.12 = (bf16[8,1,768]{2,1,0:T(2,128)(2,1)S(1)}, bf16[8,1,768]{2,1,0:T(2,128)(2,1)S(1)}, u32[]{:S(2)}, u32[]{:S(2)}) collective-permute-start(bf16[8,1,768]{2,1,0:T(2,128)(2,1)S(1)} %get-tuple-element.23), channel_id=1, source_target_pairs={{0,4},{4,8},{8,12},{12,16},{16,20},{20,24},{24,28},{1,5},{5,9},{9,... | collective-permute-start | bytes 36872 | tf_op jit(solution)/shard_map/ppermute | solution.py:17
  84.3 1.3 collective-permute-start.13
  85.6 4.5 %collective-permute-start.4 = (bf16[8,1,768]{2,1,0:T(2,128)(2,1)S(1)}, bf16[8,1,768]{2,1,0:T(2,128)(2,1)S(1)}, u32[]{:S(2)}, u32[]{:S(2)}) collective-permute-start(bf16[8,1,768]{2,1,0:T(2,128)(2,1)S(1)} %get-tuple-element.25), channel_id=1, source_target_pairs={{0,4},{4,8},{8,12},{12,16},{16,20},{20,24},{24,28},{1,5},{5,9},{9,... | collective-permute-start | bytes 36872 | tf_op jit(solution)/shard_map/ppermute | solution.py:17
  90.2 1.3 collective-permute-start.5
  91.5 0.1 multiply_convert_fusion
  91.7 3.6 %fusion.2 = f32[3,3,3,96,96]{4,3,2,1,0:T(8,128)S(1)} fusion(bf16[96,10,10,10,1]{0,3,4,2,1:T(8,128)(2,1)S(1)} %get-tuple-element.11, bf16[8,8,8,1,96]{4,2,1,0,3:T(8,128)(2,1)S(1)} %multiply_convert_fusion), kind=kOutput, calls=%fused_computation.10 | convolution fusion | flops 254803968 | bytes 1285632 | tf_op jit(solution)/shard_map/transpose | solution.py:78
  95.2 1.4 copy.49
  96.6 5.1 %collective-permute-start.14 = (bf16[1,10,768]{2,1,0:T(8,128)(2,1)S(1)}, bf16[1,10,768]{2,1,0:T(8,128)(2,1)S(1)}, u32[]{:S(2)}, u32[]{:S(2)}) collective-permute-start(bf16[1,10,768]{2,1,0:T(8,128)(2,1)S(1)} %get-tuple-element.15), channel_id=1, source_target_pairs={{0,1},{1,2},{2,3},{4,5},{5,6},{6,7},{8,9},{9,10},{10,11},{12,13},{... | collective-permute-start | bytes 46088 | tf_op jit(solution)/shard_map/ppermute | solution.py:17
  101.8 1.3 collective-permute-start.15
  103.1 5.1 %collective-permute-start.6 = (bf16[1,10,768]{2,1,0:T(8,128)(2,1)S(1)}, bf16[1,10,768]{2,1,0:T(8,128)(2,1)S(1)}, u32[]{:S(2)}, u32[]{:S(2)}) collective-permute-start(bf16[1,10,768]{2,1,0:T(8,128)(2,1)S(1)} %get-tuple-element.17), channel_id=1, source_target_pairs={{0,1},{1,2},{2,3},{4,5},{5,6},{6,7},{8,9},{9,10},{10,11},{12,13},{... | collective-permute-start | bytes 46088 | tf_op jit(solution)/shard_map/ppermute | solution.py:17
  108.2 1.5 collective-permute-start.7
  109.9 0.3 reshape.257
  110.2 2.4 collective-permute-done.7
  112.7 0.3 reshape.254
  113.1 0.1 pad_bitcast_fusion
  113.2 4.9 %fusion = f32[3,3,3,96,128]{4,3,2,1,0:T(8,128)} fusion(bf16[96,10,10,10,1]{0,3,4,2,1:T(8,128)(2,1)S(1)} %get-tuple-element.9, pred[8,8,8]{2,1,0:T(8,128)(4,1)S(1)} %broadcast_compare_fusion, bf16[8,8,8,1,128]{4,1,2,0,3:T(8,128)(2,1)S(1)} %bitcast.72), kind=kOutput, calls=%fused_computation.8 | convolution fusion | flops 339804160 | bytes 1650688 | tf_op jit(solution)/shard_map/transpose | solution.py:78
  118.1 1.1 copy-done.3
  119.2 5.5 %fusion.4 = f32[1,8,8,8,96]{4,0,3,2,1:T(1,128)S(1)} fusion(bf16[3,3,3,96,96]{4,3,2,1,0:T(8,128)(2,1)S(1)} %bitcast.67, bf16[1,10,10,10,96]{4,3,2,1,0:T(8,128)(2,1)S(1)} %pad_bitcast_fusion.4), kind=kOutput, calls=%fused_computation.12 | convolution fusion | flops 254803968 | bytes 886272 | tf_op jit(solution)/shard_map/conv_general_dilated | solution.py:54
  124.7 1.0 gather_fusion
  125.8 0.9 broadcast_divide_fusion
  126.6 6.4 %all-to-all-start.2 = ((f32[8,64,96]{2,1,0:T(8,128)}), f32[8,64,96]{2,1,0:T(8,128)S(1)}, u32[]{:S(2)}, u32[]{:S(2)}) async-start(f32[8,64,96]{2,1,0:T(8,128)} %broadcast_divide_fusion), calls=%async_computation.2 | async-start | bytes 524288 | tf_op jit(solution)/shard_map/all_to_all | solution.py:146
  133.1 3.4 %convolution_reduce_fusion = f32[8,8,8,128]{3,2,1,0:T(8,128)S(1)} fusion(bf16[3,3,3,96,128]{4,3,2,1,0:T(8,128)(2,1)S(1)} %bitcast.60, bf16[1,10,10,10,96]{4,3,2,1,0:T(8,128)(2,1)S(1)} %get-tuple-element.10), kind=kOutput, calls=%fused_computation.4 | convolution fusion | flops 339738624 | bytes 1117696 | tf_op jit(solution)/shard_map/conv_general_dilated | solution.py:54
  136.6 0.8 fusion.14
  137.3 6.9 %all-to-all-done.2 = f32[8,64,96]{2,1,0:T(8,128)S(1)} async-done(((f32[8,64,96]{2,1,0:T(8,128)}), f32[8,64,96]{2,1,0:T(8,128)S(1)}, u32[]{:S(2)}, u32[]{:S(2)}) %all-to-all-start.2) | async-done | bytes 196640 | tf_op jit(solution)/shard_map/all_to_all | solution.py:146
  144.4 0.3 convolution_bitcast_fusion
  144.7 0.6 slice.119
  145.3 0.6 slice_reduce_fusion
  146.0 113.4 %all-reduce.8.cloned.1.call-done = (f32[2592,96]{0,1:T(8,128)}, f32[2592,128]{1,0:T(8,128)}) async-done(((f32[2592,96]{0,1:T(8,128)}, f32[2592,128]{1,0:T(8,128)}), (f32[2592,96]{0,1:T(8,128)}, f32[2592,128]{1,0:T(8,128)})) %all-reduce.8.cloned.1.call-update) | async-done | bytes 2322448 | tf_op jit(solution)/shard_map/psum | solution.py:142
  259.4 2.3 copy.77
  261.7 1.1 copy.78
  (74 shorter events, 2.6 us)
Async XLA Ops:
  7.2 64.3 %copy-start = (bf16[2592,128]{1,0:T(8,128)(2,1)S(1)}, bf16[2592,128]{1,0:T(8,128)(2,1)}, u32[]{:S(2)}) copy-start(bf16[2592,128]{1,0:T(8,128)(2,1)} %param.20) | copy-start | bytes 1990660
  7.2 17.0 %copy-start.4 = (bf16[2592,96]{0,1:T(8,128)(2,1)S(1)}, bf16[2592,96]{0,1:T(8,128)(2,1)}, u32[]{:S(2)}) copy-start(bf16[2592,96]{0,1:T(8,128)(2,1)} %param.19) | copy-start | bytes 1492996
  9.4 15.2 %all-to-all-start = ((s32[8,1,64]{2,1,0:T(1,128)}), s32[8,1,64]{2,1,0:T(1,128)S(1)}, u32[]{:S(2)}, u32[]{:S(2)}) async-start(s32[8,1,64]{2,1,0:T(1,128)} %compare_select_fusion), calls=%async_computation | async-start | bytes 8192 | tf_op jit(solution)/shard_map/all_to_all | solution.py:117
  21.6 14.7 %copy-start.5 = (bf16[8,8,1024]{2,1,0:T(8,128)(2,1)S(1)}, bf16[8,8,1024]{2,1,0:T(8,128)(2,1)}, u32[]{:S(2)}) copy-start(bf16[8,8,1024]{2,1,0:T(8,128)(2,1)} %param.21) | copy-start | bytes 393220
  24.5 52.1 %copy-start.2 = (bf16[2592,96]{1,0:T(8,128)(2,1)}, bf16[2592,96]{1,0:T(8,128)(2,1)S(1)}, u32[]{:S(2)}) copy-start(bf16[2592,96]{1,0:T(8,128)(2,1)S(1)} %copy.40) | copy-start | bytes 1492996
  24.5 28.5 %all-to-all-start.1 = ((bf16[8,64,96]{2,1,0:T(8,128)(2,1)}), bf16[8,64,96]{2,1,0:T(8,128)(2,1)S(1)}, u32[]{:S(2)}, u32[]{:S(2)}) async-start(bf16[8,64,96]{2,1,0:T(8,128)(2,1)} %bitcast.7), calls=%async_computation.1 | async-start | bytes 262144 | tf_op jit(solution)/shard_map/all_to_all | solution.py:116
  30.5 228.8 %all-reduce.8.cloned.1.call-start = ((), (), s32[]{:S(2)}) async-start(), calls=%async_computation.3 | async-start | bytes 4718592 | tf_op jit(solution)/shard_map/psum | solution.py:142
  36.5 5.5 %collective-permute-start.8 = (bf16[8,1,1024]{2,1,0:T(2,128)(2,1)S(1)}, bf16[8,1,1024]{2,1,0:T(2,128)(2,1)S(1)}, u32[]{:S(2)}, u32[]{:S(2)}) collective-permute-start(bf16[8,1,1024]{2,1,0:T(2,128)(2,1)S(1)} %get-tuple-element.21), channel_id=1, source_target_pairs={{0,4},{4,8},{8,12},{12,16},{16,20},{20,24},{24,28},{1,5},{5,9},{9,... | collective-permute-start | bytes 49160 | tf_op jit(solution)/shard_map/ppermute | solution.py:17
  40.3 5.8 %collective-permute-start.9 = (bf16[8,1,1024]{2,1,0:T(2,128)(2,1)S(1)}, bf16[8,1,1024]{2,1,0:T(2,128)(2,1)S(1)}, u32[]{:S(2)}, u32[]{:S(2)}) collective-permute-start(bf16[8,1,1024]{2,1,0:T(2,128)(2,1)S(1)} %get-tuple-element.22), channel_id=1, source_target_pairs={{4,0},{8,4},{12,8},{16,12},{20,16},{24,20},{28,24},{5,1},{9,5},{13... | collective-permute-start | bytes 49160 | tf_op jit(solution)/shard_map/ppermute | solution.py:19
  41.7 10.8 %copy-start.8 = (s32[1024]{0:T(1024)}, s32[1024]{0:T(1024)S(1)}, u32[]{:S(2)}) copy-start(s32[1024]{0:T(1024)S(1)} %pad_clamp_fusion) | copy-start | bytes 12292
  46.2 6.5 %collective-permute-start.10 = (bf16[1,10,1024]{2,1,0:T(8,128)(2,1)S(1)}, bf16[1,10,1024]{2,1,0:T(8,128)(2,1)S(1)}, u32[]{:S(2)}, u32[]{:S(2)}) collective-permute-start(bf16[1,10,1024]{2,1,0:T(8,128)(2,1)S(1)} %get-tuple-element.13), channel_id=1, source_target_pairs={{0,1},{1,2},{2,3},{4,5},{5,6},{6,7},{8,9},{9,10},{10,11},{12,13},{... | collective-permute-start | bytes 61448 | tf_op jit(solution)/shard_map/ppermute | solution.py:17
  47.5 5.2 %collective-permute-start.11 = (bf16[1,10,1024]{2,1,0:T(8,128)(2,1)S(1)}, bf16[1,10,1024]{2,1,0:T(8,128)(2,1)S(1)}, u32[]{:S(2)}, u32[]{:S(2)}) collective-permute-start(bf16[1,10,1024]{2,1,0:T(8,128)(2,1)S(1)} %get-tuple-element.14), channel_id=1, source_target_pairs={{1,0},{2,1},{3,2},{5,4},{6,5},{7,6},{9,8},{10,9},{11,10},{13,12},{... | collective-permute-start | bytes 61448 | tf_op jit(solution)/shard_map/ppermute | solution.py:19
  56.6 5.3 %collective-permute-start = (bf16[8,1,768]{2,1,0:T(2,128)(2,1)S(1)}, bf16[8,1,768]{2,1,0:T(2,128)(2,1)S(1)}, u32[]{:S(2)}, u32[]{:S(2)}) collective-permute-start(bf16[8,1,768]{2,1,0:T(2,128)(2,1)S(1)} %get-tuple-element.27), channel_id=1, source_target_pairs={{0,4},{4,8},{8,12},{12,16},{16,20},{20,24},{24,28},{1,5},{5,9},{9,... | collective-permute-start | bytes 36872 | tf_op jit(solution)/shard_map/ppermute | solution.py:17
  60.4 5.7 %collective-permute-start.1 = (bf16[8,1,768]{2,1,0:T(2,128)(2,1)S(1)}, bf16[8,1,768]{2,1,0:T(2,128)(2,1)S(1)}, u32[]{:S(2)}, u32[]{:S(2)}) collective-permute-start(bf16[8,1,768]{2,1,0:T(2,128)(2,1)S(1)} %get-tuple-element.28), channel_id=1, source_target_pairs={{4,0},{8,4},{12,8},{16,12},{20,16},{24,20},{28,24},{5,1},{9,5},{13... | collective-permute-start | bytes 36872 | tf_op jit(solution)/shard_map/ppermute | solution.py:19
  66.2 10.0 %collective-permute-start.2 = (bf16[1,10,768]{2,1,0:T(8,128)(2,1)S(1)}, bf16[1,10,768]{2,1,0:T(8,128)(2,1)S(1)}, u32[]{:S(2)}, u32[]{:S(2)}) collective-permute-start(bf16[1,10,768]{2,1,0:T(8,128)(2,1)S(1)} %get-tuple-element.19), channel_id=1, source_target_pairs={{0,1},{1,2},{2,3},{4,5},{5,6},{6,7},{8,9},{9,10},{10,11},{12,13},{... | collective-permute-start | bytes 46088 | tf_op jit(solution)/shard_map/ppermute | solution.py:17
  70.0 6.2 %collective-permute-start.3 = (bf16[1,10,768]{2,1,0:T(8,128)(2,1)S(1)}, bf16[1,10,768]{2,1,0:T(8,128)(2,1)S(1)}, u32[]{:S(2)}, u32[]{:S(2)}) collective-permute-start(bf16[1,10,768]{2,1,0:T(8,128)(2,1)S(1)} %get-tuple-element.20), channel_id=1, source_target_pairs={{1,0},{2,1},{3,2},{5,4},{6,5},{7,6},{9,8},{10,9},{11,10},{13,12},{... | collective-permute-start | bytes 46088 | tf_op jit(solution)/shard_map/ppermute | solution.py:19
  81.1 15.5 %collective-permute-start.12 = (bf16[8,1,768]{2,1,0:T(2,128)(2,1)S(1)}, bf16[8,1,768]{2,1,0:T(2,128)(2,1)S(1)}, u32[]{:S(2)}, u32[]{:S(2)}) collective-permute-start(bf16[8,1,768]{2,1,0:T(2,128)(2,1)S(1)} %get-tuple-element.23), channel_id=1, source_target_pairs={{0,4},{4,8},{8,12},{12,16},{16,20},{20,24},{24,28},{1,5},{5,9},{9,... | collective-permute-start | bytes 36872 | tf_op jit(solution)/shard_map/ppermute | solution.py:17
  84.3 12.3 %collective-permute-start.13 = (bf16[8,1,768]{2,1,0:T(2,128)(2,1)S(1)}, bf16[8,1,768]{2,1,0:T(2,128)(2,1)S(1)}, u32[]{:S(2)}, u32[]{:S(2)}) collective-permute-start(bf16[8,1,768]{2,1,0:T(2,128)(2,1)S(1)} %get-tuple-element.24), channel_id=1, source_target_pairs={{4,0},{8,4},{12,8},{16,12},{20,16},{24,20},{28,24},{5,1},{9,5},{13... | collective-permute-start | bytes 36872 | tf_op jit(solution)/shard_map/ppermute | solution.py:19
  85.6 17.4 %collective-permute-start.4 = (bf16[8,1,768]{2,1,0:T(2,128)(2,1)S(1)}, bf16[8,1,768]{2,1,0:T(2,128)(2,1)S(1)}, u32[]{:S(2)}, u32[]{:S(2)}) collective-permute-start(bf16[8,1,768]{2,1,0:T(2,128)(2,1)S(1)} %get-tuple-element.25), channel_id=1, source_target_pairs={{0,4},{4,8},{8,12},{12,16},{16,20},{20,24},{24,28},{1,5},{5,9},{9,... | collective-permute-start | bytes 36872 | tf_op jit(solution)/shard_map/ppermute | solution.py:17
  90.2 12.9 %collective-permute-start.5 = (bf16[8,1,768]{2,1,0:T(2,128)(2,1)S(1)}, bf16[8,1,768]{2,1,0:T(2,128)(2,1)S(1)}, u32[]{:S(2)}, u32[]{:S(2)}) collective-permute-start(bf16[8,1,768]{2,1,0:T(2,128)(2,1)S(1)} %get-tuple-element.26), channel_id=1, source_target_pairs={{4,0},{8,4},{12,8},{16,12},{20,16},{24,20},{28,24},{5,1},{9,5},{13... | collective-permute-start | bytes 36872 | tf_op jit(solution)/shard_map/ppermute | solution.py:19
  96.6 13.1 %collective-permute-start.14 = (bf16[1,10,768]{2,1,0:T(8,128)(2,1)S(1)}, bf16[1,10,768]{2,1,0:T(8,128)(2,1)S(1)}, u32[]{:S(2)}, u32[]{:S(2)}) collective-permute-start(bf16[1,10,768]{2,1,0:T(8,128)(2,1)S(1)} %get-tuple-element.15), channel_id=1, source_target_pairs={{0,1},{1,2},{2,3},{4,5},{5,6},{6,7},{8,9},{9,10},{10,11},{12,13},{... | collective-permute-start | bytes 46088 | tf_op jit(solution)/shard_map/ppermute | solution.py:17
  101.8 8.0 %collective-permute-start.15 = (bf16[1,10,768]{2,1,0:T(8,128)(2,1)S(1)}, bf16[1,10,768]{2,1,0:T(8,128)(2,1)S(1)}, u32[]{:S(2)}, u32[]{:S(2)}) collective-permute-start(bf16[1,10,768]{2,1,0:T(8,128)(2,1)S(1)} %get-tuple-element.16), channel_id=1, source_target_pairs={{1,0},{2,1},{3,2},{5,4},{6,5},{7,6},{9,8},{10,9},{11,10},{13,12},{... | collective-permute-start | bytes 46088 | tf_op jit(solution)/shard_map/ppermute | solution.py:19
  103.1 7.0 %collective-permute-start.6 = (bf16[1,10,768]{2,1,0:T(8,128)(2,1)S(1)}, bf16[1,10,768]{2,1,0:T(8,128)(2,1)S(1)}, u32[]{:S(2)}, u32[]{:S(2)}) collective-permute-start(bf16[1,10,768]{2,1,0:T(8,128)(2,1)S(1)} %get-tuple-element.17), channel_id=1, source_target_pairs={{0,1},{1,2},{2,3},{4,5},{5,6},{6,7},{8,9},{9,10},{10,11},{12,13},{... | collective-permute-start | bytes 46088 | tf_op jit(solution)/shard_map/ppermute | solution.py:17
  108.2 4.3 %collective-permute-start.7 = (bf16[1,10,768]{2,1,0:T(8,128)(2,1)S(1)}, bf16[1,10,768]{2,1,0:T(8,128)(2,1)S(1)}, u32[]{:S(2)}, u32[]{:S(2)}) collective-permute-start(bf16[1,10,768]{2,1,0:T(8,128)(2,1)S(1)} %get-tuple-element.18), channel_id=1, source_target_pairs={{1,0},{2,1},{3,2},{5,4},{6,5},{7,6},{9,8},{10,9},{11,10},{13,12},{... | collective-permute-start | bytes 46088 | tf_op jit(solution)/shard_map/ppermute | solution.py:19
  118.1 1.1 copy-start.3
  119.2 5.5 %copy-start.9 = (s32[1024]{0:T(1024)S(1)}, s32[1024]{0:T(1024)}, u32[]{:S(2)}) copy-start(s32[1024]{0:T(1024)} %copy-done.8) | copy-start | bytes 12292
  124.7 1.1 copy-start.7
  126.6 17.7 %all-to-all-start.2 = ((f32[8,64,96]{2,1,0:T(8,128)}), f32[8,64,96]{2,1,0:T(8,128)S(1)}, u32[]{:S(2)}, u32[]{:S(2)}) async-start(f32[8,64,96]{2,1,0:T(8,128)} %broadcast_divide_fusion), calls=%async_computation.2 | async-start | bytes 524288 | tf_op jit(solution)/shard_map/all_to_all | solution.py:146
  133.1 3.5 %copy-start.6 = (f32[8,8,8]{1,2,0:T(8,128)S(1)}, f32[8,8,8]{1,2,0:T(8,128)}, u32[]{:S(2)}) copy-start(f32[8,8,8]{1,2,0:T(8,128)} %copy.38) | copy-start | bytes 6148
  136.5 7.9 %copy-start.10 = (f32[8,96]{1,0:T(8,128)S(1)}, f32[8,96]{1,0:T(8,128)}, u32[]{:S(2)}) copy-start(f32[8,96]{1,0:T(8,128)} %param.17) | copy-start | bytes 9220
  136.5 7.9 %copy-start.11 = (f32[512,96]{0,1:T(8,128)S(1)}, f32[512,96]{0,1:T(8,128)}, u32[]{:S(2)}) copy-start(f32[512,96]{0,1:T(8,128)} %get-tuple-element.36) | copy-start | bytes 589828
  259.4 2.4 copy-start.1
Sparse Core Ops, SparseCore 0:
  118.2 141.0 all-reduce.7
where the time goes:
time: 271 us; the launch traced here: 270 us
  waiting for transfers between devices  132 us (49%)
  starting transfers between devices  61.3 us (23%)
  matrix products  27.6 us (10%)
  local copies, waits for them, and re-layouts  18.2 us (7%)
  between operations  15.5 us (6%)
  other arithmetic  15.4 us (6%)
    psum x1, waiting for transfers between devices, shards(): one_total, two_total = lax.psum((part_one, part_two), ('blk', 'rep'))  113 us
    ppermute x8, starting transfers between devices, with_halo(): lax.ppermute(tail, axis, [(i, (i + 1) % count) for i in range(ends)])  30.7 us
    conv_general_dilated x4, matrix products, conv_apply(): lax.conv_general_dilated(padded[None], kernel, (1, 1, 1), 'VALID', dimens...  17 us
    ppermute x8, waiting for transfers between devices, with_halo(): lax.ppermute(head, axis, [((i + 1) % count, i) for i in range(ends)])  10.9 us
    ppermute x8, starting transfers between devices, with_halo(): lax.ppermute(head, axis, [((i + 1) % count, i) for i in range(ends)])  10.7 us
    transpose x2, matrix products, kernel_grad(): jnp.transpose(result, (1, 2, 3, 0, 4))  8.46 us
    all_to_all x1, starting transfers between devices, shards(): lax.all_to_all(vox_sent, 'blk', split_axis=0, concat_axis=0, tiled=True)  7.31 us
    all_to_all x1, waiting for transfers between devices, shards(): lax.all_to_all(grad_feat.reshape(owners, SLOT_CAP, width_one), 'blk', spl...  6.94 us
  transfers between devices with their start and end apart: 20, of which 7 were waited for; matrix products, arithmetic and copies ran while one was open for 15% of the time, Pallas kernels for 0%

commit v1 on v0

--- a/solution.py
+++ b/solution.py
@@ -139,7 +139,7 @@
     grad_act_pad = with_faces(grad_act.reshape(edge_len, edge_len, -1), width_one)
     grad_pooled = conv_apply(grad_act_pad, flipped(conv_one, width_one), width_one)
     part_one = kernel_grad(pooled_pad, grad_act, edge_len)
-    one_total, two_total = lax.psum((part_one, part_two), ("blk", "rep"))
+    one_total, two_total = lax.psum(lax.psum((part_one, part_two), "rep"), "blk")
     grad_ext = jnp.concatenate([grad_pooled, jnp.zeros((1, width_one), jnp.float32)], axis=0)
     count_ext = jnp.concatenate([divisor, jnp.ones((1,), jnp.float32)])
     grad_feat = grad_ext[vox_flat] / count_ext[vox_flat][:, None]

time: 271 us -> 291 us (1.074)
  waiting for transfers between devices: 132 us -> 161 us
  starting transfers between devices: 61.3 us -> 52.2 us
    psum x1 -> x2, waiting for transfers between devices: 113 us -> 134 us  [the longest x1 79.3 us: shards(): lax.psum(lax.psum((part_one, part_two), 'rep'), 'blk')]
    ppermute x8, starting transfers between devices: 30.7 us -> 21.6 us  [with_halo(): lax.ppermute(tail, axis, [(i, (i + 1) % count) for i in range(ends)])]
    all_to_all x1, waiting for transfers between devices: 6.94 us -> 13.5 us  [shards(): lax.all_to_all(grad_feat.reshape(owners, SLOT_CAP, width_one), 'blk', spl...]
  transfers between devices with their start and end apart: 20 -> 21, of which waited for: 7 -> 9; matrix products, arithmetic and copies ran while one was open for 15% -> 12% of each run, Pallas kernels for 0% -> 0%
where the time goes in v1:
time: 291 us; the launch traced here: 290 us
  waiting for transfers between devices  161 us (55%)
  starting transfers between devices  52.2 us (18%)
  matrix products  27.5 us (9%)
  local copies, waits for them, and re-layouts  17.1 us (6%)
  other arithmetic  16.9 us (6%)
  between operations  15.5 us (5%)
    psum x1, waiting for transfers between devices, shards(): lax.psum(lax.psum((part_one, part_two), 'rep'), 'blk')  79.3 us
    psum x1, waiting for transfers between devices, shards(): lax.psum((part_one, part_two), 'rep')  54.3 us
    ppermute x8, starting transfers between devices, with_halo(): lax.ppermute(tail, axis, [(i, (i + 1) % count) for i in range(ends)])  21.6 us
    conv_general_dilated x4, matrix products, conv_apply(): lax.conv_general_dilated(padded[None], kernel, (1, 1, 1), 'VALID', dimens...  17.1 us
    all_to_all x1, waiting for transfers between devices, shards(): lax.all_to_all(grad_feat.reshape(owners, SLOT_CAP, width_one), 'blk', spl...  13.5 us
    ppermute x8, waiting for transfers between devices, with_halo(): lax.ppermute(head, axis, [((i + 1) % count, i) for i in range(ends)])  11.9 us
    ppermute x8, starting transfers between devices, with_halo(): lax.ppermute(head, axis, [((i + 1) % count, i) for i in range(ends)])  11 us
    transpose x2, matrix products, kernel_grad(): jnp.transpose(result, (1, 2, 3, 0, 4))  8.36 us
  transfers between devices with their start and end apart: 21, of which 9 were waited for; matrix products, arithmetic and copies ran while one was open for 12% of the time, Pallas kernels for 0%

profile of v1, /device:TPU:0, one launch (start us, length us, event | category | flops | bytes accessed | tf_op | source)
XLA Modules:
  0.0 290.4 jit_solution(6332117913405881907)
XLA Ops:
  7.2 0.9 reshape.249
  8.0 1.3 compare_select_fusion
  9.4 7.3 %all-to-all-start = ((s32[8,1,64]{2,1,0:T(1,128)}), s32[8,1,64]{2,1,0:T(1,128)S(1)}, u32[]{:S(2)}, u32[]{:S(2)}) async-start(s32[8,1,64]{2,1,0:T(1,128)} %compare_select_fusion), calls=%async_computation | async-start | bytes 8192 | tf_op jit(solution)/shard_map/all_to_all | solution.py:117
  17.5 1.4 fusion.41
  18.8 2.8 subtract_add_fusion
  21.6 1.5 all-to-all-done
  23.1 0.5 broadcast.171
  23.6 0.7 reduce.15
  24.4 4.1 %scatter_custom_fusion = s32[513]{0:T(1024)S(1)} fusion(s32[512]{0:T(512)S(1)} %reshape.282, s32[512]{0:T(512)S(1)} %broadcast.146, s32[]{:T(128)} %constant.8.clone.1), kind=kCustom, calls=%fused_computation.82 | custom fusion | flops 512 | bytes 2056 | tf_op jit(solution)/shard_map/scatter-add | solution.py:121
  28.7 1.0 bitcast_select_fusion
  29.8 2.5 collective-permute-start.8
  32.2 1.3 collective-permute-start.9
  33.5 1.8 multiply_convert_fusion.3
  35.3 0.8 copy.39
  36.1 6.6 %all-to-all-start.1 = ((bf16[8,64,96]{2,1,0:T(8,128)(2,1)}), bf16[8,64,96]{2,1,0:T(8,128)(2,1)S(1)}, u32[]{:S(2)}, u32[]{:S(2)}) async-start(bf16[8,64,96]{2,1,0:T(8,128)(2,1)} %bitcast.7), calls=%async_computation.1 | async-start | bytes 262144 | tf_op jit(solution)/shard_map/all_to_all | solution.py:116
  42.8 0.3 copy.40
  43.2 1.3 collective-permute-start.10
  44.5 1.3 collective-permute-start.11
  46.1 3.2 %collective-permute-done.11 = bf16[1,10,1024]{2,1,0:T(8,128)(2,1)S(1)} collective-permute-done((bf16[1,10,1024]{2,1,0:T(8,128)(2,1)S(1)}, bf16[1,10,1024]{2,1,0:T(8,128)(2,1)S(1)}, u32[]{:S(2)}, u32[]{:S(2)}) %collective-permute-start.11) | collective-permute-done | bytes 20512 | tf_op jit(solution)/shard_map/ppermute | solution.py:19
  49.6 0.5 all-to-all-done.1
  50.1 3.2 %scatter_custom_fusion.1 = f32[513,96]{1,0:T(8,128)S(1)} fusion(s32[512]{0:T(512)S(1)} %reshape.282, bf16[512,96]{1,0:T(8,128)(2,1)S(1)} %bitcast.68, f32[]{:T(128)} %constant.11.clone.1), kind=kCustom, calls=%fused_computation.28 | custom fusion | flops 98304 | bytes 328068 | tf_op jit(solution)/shard_map/scatter-add | solution.py:123
  53.3 0.1 fusion.11
  53.6 3.0 %collective-permute-start = (bf16[8,1,768]{2,1,0:T(2,128)(2,1)S(1)}, bf16[8,1,768]{2,1,0:T(2,128)(2,1)S(1)}, u32[]{:S(2)}, u32[]{:S(2)}) collective-permute-start(bf16[8,1,768]{2,1,0:T(2,128)(2,1)S(1)} %get-tuple-element.29), channel_id=1, source_target_pairs={{0,4},{4,8},{8,12},{12,16},{16,20},{20,24},{24,28},{1,5},{5,9},{9,... | collective-permute-start | bytes 36872 | tf_op jit(solution)/shard_map/ppermute | solution.py:17
  56.6 1.3 collective-permute-start.1
  58.1 4.4 %collective-permute-done.1 = bf16[8,1,768]{2,1,0:T(2,128)(2,1)S(1)} collective-permute-done((bf16[8,1,768]{2,1,0:T(2,128)(2,1)S(1)}, bf16[8,1,768]{2,1,0:T(2,128)(2,1)S(1)}, u32[]{:S(2)}, u32[]{:S(2)}) %collective-permute-start.1) | collective-permute-done | bytes 12320 | tf_op jit(solution)/shard_map/ppermute | solution.py:19
  62.6 3.4 %collective-permute-start.2 = (bf16[1,10,768]{2,1,0:T(8,128)(2,1)S(1)}, bf16[1,10,768]{2,1,0:T(8,128)(2,1)S(1)}, u32[]{:S(2)}, u32[]{:S(2)}) collective-permute-start(bf16[1,10,768]{2,1,0:T(8,128)(2,1)S(1)} %get-tuple-element.21), channel_id=1, source_target_pairs={{0,1},{1,2},{2,3},{4,5},{5,6},{6,7},{8,9},{9,10},{10,11},{12,13},{... | collective-permute-start | bytes 46088 | tf_op jit(solution)/shard_map/ppermute | solution.py:17
  65.9 1.5 collective-permute-start.3
  67.4 0.5 broadcast.172
  67.9 4.0 %fusion.43 = (f32[8,8,8,96]{3,2,1,0:T(8,128)S(1)}, f32[1,8,8,8,96]{4,0,3,2,1:T(1,128)S(1)}) fusion(f32[]{:T(128)} %broadcast.172, bf16[3,3,3,96,128]{4,3,2,1,0:T(8,128)(2,1)S(1)} %bitcast.61, bf16[1,10,10,10,128]{4,3,2,1,0:T(8,128)(2,1)S(1)} %pad_bitcast_fusion.5), kind=kOutput, calls=%fused_computation.94 | convolution fusion | flops 339738624 | bytes 1312772 | tf_op jit(solution)/shard_map/conv_general_dilated | solution.py:54
  72.2 0.3 reshape.252
  72.6 4.1 %fusion.42 = (f32[8,8,8,96]{3,2,1,0:T(8,128)S(1)}, f32[1,8,8,8,96]{4,0,3,2,1:T(1,128)S(1)}) fusion(f32[]{:T(128)} %broadcast.172, bf16[3,3,3,96,96]{4,3,2,1,0:T(8,128)(2,1)S(1)} %bitcast.66, bf16[1,10,10,10,96]{4,3,2,1,0:T(8,128)(2,1)S(1)} %get-tuple-element.14), kind=kOutput, calls=%fused_computation.93 | convolution fusion | flops 254803968 | bytes 1082884 | tf_op jit(solution)/shard_map/conv_general_dilated | solution.py:54
  76.9 0.7 multiply_convert_fusion.1
  77.7 4.1 %collective-permute-start.4 = (bf16[8,1,768]{2,1,0:T(2,128)(2,1)S(1)}, bf16[8,1,768]{2,1,0:T(2,128)(2,1)S(1)}, u32[]{:S(2)}, u32[]{:S(2)}) collective-permute-start(bf16[8,1,768]{2,1,0:T(2,128)(2,1)S(1)} %get-tuple-element.27), channel_id=1, source_target_pairs={{0,4},{4,8},{8,12},{12,16},{16,20},{20,24},{24,28},{1,5},{5,9},{9,... | collective-permute-start | bytes 36872 | tf_op jit(solution)/shard_map/ppermute | solution.py:17
  81.7 1.3 collective-permute-start.5
  83.0 0.1 multiply_convert_fusion
  83.2 4.2 %collective-permute-done.5 = bf16[8,1,768]{2,1,0:T(2,128)(2,1)S(1)} collective-permute-done((bf16[8,1,768]{2,1,0:T(2,128)(2,1)S(1)}, bf16[8,1,768]{2,1,0:T(2,128)(2,1)S(1)}, u32[]{:S(2)}, u32[]{:S(2)}) %collective-permute-start.5) | collective-permute-done | bytes 12320 | tf_op jit(solution)/shard_map/ppermute | solution.py:19
  87.5 2.8 collective-permute-start.6
  90.3 1.5 collective-permute-start.7
  91.8 3.5 %fusion.2 = f32[3,3,3,96,96]{4,3,2,1,0:T(8,128)S(1)} fusion(bf16[96,10,10,10,1]{0,3,4,2,1:T(8,128)(2,1)S(1)} %get-tuple-element.13, bf16[8,8,8,1,96]{4,2,1,0,3:T(8,128)(2,1)S(1)} %multiply_convert_fusion), kind=kOutput, calls=%fused_computation.10 | convolution fusion | flops 254803968 | bytes 1285632 | tf_op jit(solution)/shard_map/transpose | solution.py:78
  95.3 1.4 copy.49
  96.8 0.3 reshape.254
  97.3 0.4 copy-done.8
  97.6 4.8 %fusion = f32[3,3,3,96,128]{4,3,2,1,0:T(8,128)} fusion(bf16[96,10,10,10,1]{0,3,4,2,1:T(8,128)(2,1)S(1)} %get-tuple-element.11, pred[8,8,8]{2,1,0:T(8,128)(4,1)S(1)} %broadcast_compare_fusion, bf16[8,8,8,1,128]{4,1,2,0,3:T(8,128)(2,1)S(1)} %bitcast.72), kind=kOutput, calls=%fused_computation.8 | convolution fusion | flops 339804160 | bytes 1650688 | tf_op jit(solution)/shard_map/transpose | solution.py:78
  102.5 0.6 copy-done.10
  103.4 3.2 %collective-permute-start.12 = (bf16[8,1,768]{2,1,0:T(2,128)(2,1)S(1)}, bf16[8,1,768]{2,1,0:T(2,128)(2,1)S(1)}, u32[]{:S(2)}, u32[]{:S(2)}) collective-permute-start(bf16[8,1,768]{2,1,0:T(2,128)(2,1)S(1)} %get-tuple-element.25), channel_id=1, source_target_pairs={{0,4},{4,8},{8,12},{12,16},{16,20},{20,24},{24,28},{1,5},{5,9},{9,... | collective-permute-start | bytes 36872 | tf_op jit(solution)/shard_map/ppermute | solution.py:17
  106.6 1.3 collective-permute-start.13
  107.9 54.3 %all-reduce.12.cloned.1.call-done = (f32[2592,96]{0,1:T(8,128)}, f32[2592,128]{1,0:T(8,128)}) async-done(((f32[2592,96]{0,1:T(8,128)}, f32[2592,128]{1,0:T(8,128)}), (f32[2592,96]{0,1:T(8,128)}, f32[2592,128]{1,0:T(8,128)})) %all-reduce.12.cloned.1.call-update) | async-done | bytes 2322448 | tf_op jit(solution)/shard_map/psum | solution.py:142
  162.3 1.5 collective-permute-start.14
  163.9 1.6 collective-permute-start.15
  165.5 2.3 gather_fusion.1
  168.0 0.3 reshape.257
  168.4 5.5 %fusion.4 = f32[1,8,8,8,96]{4,0,3,2,1:T(1,128)S(1)} fusion(bf16[3,3,3,96,96]{4,3,2,1,0:T(8,128)(2,1)S(1)} %bitcast.67, bf16[1,10,10,10,96]{4,3,2,1,0:T(8,128)(2,1)S(1)} %pad_bitcast_fusion.4), kind=kOutput, calls=%fused_computation.12 | convolution fusion | flops 254803968 | bytes 886272 | tf_op jit(solution)/shard_map/conv_general_dilated | solution.py:54
  174.0 1.0 gather_fusion
  175.0 0.8 broadcast_divide_fusion
  175.9 5.5 %all-to-all-start.2 = ((f32[8,64,96]{2,1,0:T(8,128)}), f32[8,64,96]{2,1,0:T(8,128)S(1)}, u32[]{:S(2)}, u32[]{:S(2)}) async-start(f32[8,64,96]{2,1,0:T(8,128)} %broadcast_divide_fusion), calls=%async_computation.2 | async-start | bytes 524288 | tf_op jit(solution)/shard_map/all_to_all | solution.py:146
  181.4 3.4 %convolution_reduce_fusion = f32[8,8,8,128]{3,2,1,0:T(8,128)S(1)} fusion(bf16[3,3,3,96,128]{4,3,2,1,0:T(8,128)(2,1)S(1)} %bitcast.60, bf16[1,10,10,10,96]{4,3,2,1,0:T(8,128)(2,1)S(1)} %get-tuple-element.12), kind=kOutput, calls=%fused_computation.4 | convolution fusion | flops 339738624 | bytes 1117696 | tf_op jit(solution)/shard_map/conv_general_dilated | solution.py:54
  184.9 0.8 fusion.14
  185.7 13.5 %all-to-all-done.2 = f32[8,64,96]{2,1,0:T(8,128)S(1)} async-done(((f32[8,64,96]{2,1,0:T(8,128)}), f32[8,64,96]{2,1,0:T(8,128)S(1)}, u32[]{:S(2)}, u32[]{:S(2)}) %all-to-all-start.2) | async-done | bytes 196640 | tf_op jit(solution)/shard_map/all_to_all | solution.py:146
  199.3 0.3 convolution_bitcast_fusion
  199.6 0.6 slice.119
  200.2 0.6 slice_reduce_fusion
  200.9 79.3 %all-reduce.10.cloned.1.call-done = (f32[2592,96]{0,1:T(8,128)}, f32[2592,128]{1,0:T(8,128)}) async-done(((f32[2592,96]{0,1:T(8,128)}, f32[2592,128]{1,0:T(8,128)}), (f32[2592,96]{0,1:T(8,128)}, f32[2592,128]{1,0:T(8,128)})) %all-reduce.10.cloned.1.call-update) | async-done | bytes 2322448 | tf_op jit(solution)/shard_map/psum | solution.py:142
  280.1 2.3 copy.79
  282.5 1.1 copy.80
  (83 shorter events, 3.1 us)
Async XLA Ops:
  7.2 60.2 %copy-start = (bf16[2592,128]{1,0:T(8,128)(2,1)S(1)}, bf16[2592,128]{1,0:T(8,128)(2,1)}, u32[]{:S(2)}) copy-start(bf16[2592,128]{1,0:T(8,128)(2,1)} %param.20) | copy-start | bytes 1990660
  7.2 35.6 %copy-start.7 = (bf16[2592,96]{0,1:T(8,128)(2,1)S(1)}, bf16[2592,96]{0,1:T(8,128)(2,1)}, u32[]{:S(2)}) copy-start(bf16[2592,96]{0,1:T(8,128)(2,1)} %param.19) | copy-start | bytes 1492996
  9.4 13.7 %all-to-all-start = ((s32[8,1,64]{2,1,0:T(1,128)}), s32[8,1,64]{2,1,0:T(1,128)S(1)}, u32[]{:S(2)}, u32[]{:S(2)}) async-start(s32[8,1,64]{2,1,0:T(1,128)} %compare_select_fusion), calls=%async_computation | async-start | bytes 8192 | tf_op jit(solution)/shard_map/all_to_all | solution.py:117
  23.1 5.5 %copy-start.9 = (s32[8,1,64]{2,1,0:T(1,128)}, s32[8,1,64]{2,1,0:T(1,128)S(1)}, u32[]{:S(2)}) copy-start(s32[8,1,64]{2,1,0:T(1,128)S(1)} %all-to-all-done) | copy-start | bytes 6148
  28.6 54.5 %copy-start.3 = (f32[8,8,8]{2,1,0:T(8,128)}, f32[8,8,8]{2,1,0:T(8,128)S(1)}, u32[]{:S(2)}) copy-start(f32[8,8,8]{2,1,0:T(8,128)S(1)} %reshape.262) | copy-start | bytes 6148
  29.8 13.3 %collective-permute-start.8 = (bf16[8,1,1024]{2,1,0:T(2,128)(2,1)S(1)}, bf16[8,1,1024]{2,1,0:T(2,128)(2,1)S(1)}, u32[]{:S(2)}, u32[]{:S(2)}) collective-permute-start(bf16[8,1,1024]{2,1,0:T(2,128)(2,1)S(1)} %get-tuple-element.23), channel_id=1, source_target_pairs={{0,4},{4,8},{8,12},{12,16},{16,20},{20,24},{24,28},{1,5},{5,9},{9,... | collective-permute-start | bytes 49160 | tf_op jit(solution)/shard_map/ppermute | solution.py:17
  32.2 10.9 %collective-permute-start.9 = (bf16[8,1,1024]{2,1,0:T(2,128)(2,1)S(1)}, bf16[8,1,1024]{2,1,0:T(2,128)(2,1)S(1)}, u32[]{:S(2)}, u32[]{:S(2)}) collective-permute-start(bf16[8,1,1024]{2,1,0:T(2,128)(2,1)S(1)} %get-tuple-element.24), channel_id=1, source_target_pairs={{4,0},{8,4},{12,8},{16,12},{20,16},{24,20},{28,24},{5,1},{9,5},{13... | collective-permute-start | bytes 49160 | tf_op jit(solution)/shard_map/ppermute | solution.py:19
  36.1 14.0 %all-to-all-start.1 = ((bf16[8,64,96]{2,1,0:T(8,128)(2,1)}), bf16[8,64,96]{2,1,0:T(8,128)(2,1)S(1)}, u32[]{:S(2)}, u32[]{:S(2)}) async-start(bf16[8,64,96]{2,1,0:T(8,128)(2,1)} %bitcast.7), calls=%async_computation.1 | async-start | bytes 262144 | tf_op jit(solution)/shard_map/all_to_all | solution.py:116
  42.7 119.5 %all-reduce.12.cloned.1.call-start = ((), (), s32[]{:S(2)}) async-start(), calls=%async_computation.4 | async-start | bytes 4718592 | tf_op jit(solution)/shard_map/psum | solution.py:142
  43.1 29.5 %copy-start.5 = (bf16[2592,96]{1,0:T(8,128)(2,1)}, bf16[2592,96]{1,0:T(8,128)(2,1)S(1)}, u32[]{:S(2)}) copy-start(bf16[2592,96]{1,0:T(8,128)(2,1)S(1)} %copy.40) | copy-start | bytes 1492996
  43.2 2.9 collective-permute-start.10
  44.5 4.8 %collective-permute-start.11 = (bf16[1,10,1024]{2,1,0:T(8,128)(2,1)S(1)}, bf16[1,10,1024]{2,1,0:T(8,128)(2,1)S(1)}, u32[]{:S(2)}, u32[]{:S(2)}) collective-permute-start(bf16[1,10,1024]{2,1,0:T(8,128)(2,1)S(1)} %get-tuple-element.16), channel_id=1, source_target_pairs={{1,0},{2,1},{3,2},{5,4},{6,5},{7,6},{9,8},{10,9},{11,10},{13,12},{... | collective-permute-start | bytes 61448 | tf_op jit(solution)/shard_map/ppermute | solution.py:19
  45.8 7.6 %copy-start.11 = (f32[512]{0:T(512)}, f32[512]{0:T(512)S(1)}, u32[]{:S(2)}) copy-start(f32[512]{0:T(512)S(1)} %maximum_convert_fusion) | copy-start | bytes 6148
  53.6 4.5 %collective-permute-start = (bf16[8,1,768]{2,1,0:T(2,128)(2,1)S(1)}, bf16[8,1,768]{2,1,0:T(2,128)(2,1)S(1)}, u32[]{:S(2)}, u32[]{:S(2)}) collective-permute-start(bf16[8,1,768]{2,1,0:T(2,128)(2,1)S(1)} %get-tuple-element.29), channel_id=1, source_target_pairs={{0,4},{4,8},{8,12},{12,16},{16,20},{20,24},{24,28},{1,5},{5,9},{9,... | collective-permute-start | bytes 36872 | tf_op jit(solution)/shard_map/ppermute | solution.py:17
  56.6 5.9 %collective-permute-start.1 = (bf16[8,1,768]{2,1,0:T(2,128)(2,1)S(1)}, bf16[8,1,768]{2,1,0:T(2,128)(2,1)S(1)}, u32[]{:S(2)}, u32[]{:S(2)}) collective-permute-start(bf16[8,1,768]{2,1,0:T(2,128)(2,1)S(1)} %get-tuple-element.30), channel_id=1, source_target_pairs={{4,0},{8,4},{12,8},{16,12},{20,16},{24,20},{28,24},{5,1},{9,5},{13... | collective-permute-start | bytes 36872 | tf_op jit(solution)/shard_map/ppermute | solution.py:19
  62.6 9.5 %collective-permute-start.2 = (bf16[1,10,768]{2,1,0:T(8,128)(2,1)S(1)}, bf16[1,10,768]{2,1,0:T(8,128)(2,1)S(1)}, u32[]{:S(2)}, u32[]{:S(2)}) collective-permute-start(bf16[1,10,768]{2,1,0:T(8,128)(2,1)S(1)} %get-tuple-element.21), channel_id=1, source_target_pairs={{0,1},{1,2},{2,3},{4,5},{5,6},{6,7},{8,9},{9,10},{10,11},{12,13},{... | collective-permute-start | bytes 46088 | tf_op jit(solution)/shard_map/ppermute | solution.py:17
  65.9 6.2 %collective-permute-start.3 = (bf16[1,10,768]{2,1,0:T(8,128)(2,1)S(1)}, bf16[1,10,768]{2,1,0:T(8,128)(2,1)S(1)}, u32[]{:S(2)}, u32[]{:S(2)}) collective-permute-start(bf16[1,10,768]{2,1,0:T(8,128)(2,1)S(1)} %get-tuple-element.22), channel_id=1, source_target_pairs={{1,0},{2,1},{3,2},{5,4},{6,5},{7,6},{9,8},{10,9},{11,10},{13,12},{... | collective-permute-start | bytes 46088 | tf_op jit(solution)/shard_map/ppermute | solution.py:19
  77.7 5.6 %collective-permute-start.4 = (bf16[8,1,768]{2,1,0:T(2,128)(2,1)S(1)}, bf16[8,1,768]{2,1,0:T(2,128)(2,1)S(1)}, u32[]{:S(2)}, u32[]{:S(2)}) collective-permute-start(bf16[8,1,768]{2,1,0:T(2,128)(2,1)S(1)} %get-tuple-element.27), channel_id=1, source_target_pairs={{0,4},{4,8},{8,12},{12,16},{16,20},{20,24},{24,28},{1,5},{5,9},{9,... | collective-permute-start | bytes 36872 | tf_op jit(solution)/shard_map/ppermute | solution.py:17
  81.7 5.7 %collective-permute-start.5 = (bf16[8,1,768]{2,1,0:T(2,128)(2,1)S(1)}, bf16[8,1,768]{2,1,0:T(2,128)(2,1)S(1)}, u32[]{:S(2)}, u32[]{:S(2)}) collective-permute-start(bf16[8,1,768]{2,1,0:T(2,128)(2,1)S(1)} %get-tuple-element.28), channel_id=1, source_target_pairs={{4,0},{8,4},{12,8},{16,12},{20,16},{24,20},{28,24},{5,1},{9,5},{13... | collective-permute-start | bytes 36872 | tf_op jit(solution)/shard_map/ppermute | solution.py:19
  87.5 9.2 %collective-permute-start.6 = (bf16[1,10,768]{2,1,0:T(8,128)(2,1)S(1)}, bf16[1,10,768]{2,1,0:T(8,128)(2,1)S(1)}, u32[]{:S(2)}, u32[]{:S(2)}) collective-permute-start(bf16[1,10,768]{2,1,0:T(8,128)(2,1)S(1)} %get-tuple-element.19), channel_id=1, source_target_pairs={{0,1},{1,2},{2,3},{4,5},{5,6},{6,7},{8,9},{9,10},{10,11},{12,13},{... | collective-permute-start | bytes 46088 | tf_op jit(solution)/shard_map/ppermute | solution.py:17
  90.3 6.5 %collective-permute-start.7 = (bf16[1,10,768]{2,1,0:T(8,128)(2,1)S(1)}, bf16[1,10,768]{2,1,0:T(8,128)(2,1)S(1)}, u32[]{:S(2)}, u32[]{:S(2)}) collective-permute-start(bf16[1,10,768]{2,1,0:T(8,128)(2,1)S(1)} %get-tuple-element.20), channel_id=1, source_target_pairs={{1,0},{2,1},{3,2},{5,4},{6,5},{7,6},{9,8},{10,9},{11,10},{13,12},{... | collective-permute-start | bytes 46088 | tf_op jit(solution)/shard_map/ppermute | solution.py:19
  96.7 0.9 copy-start.8
  102.5 0.7 copy-start.10
  102.5 0.9 copy-start.2
  102.5 177.6 %all-reduce.10.cloned.1.call-start = ((), (), s32[]{:S(2)}) async-start(), calls=%async_computation.3 | async-start | bytes 4718592 | tf_op jit(solution)/shard_map/psum | solution.py:142
  103.4 62.1 %copy-start.12 = (f32[512]{0:T(512)S(1)}, f32[512]{0:T(512)}, u32[]{:S(2)}) copy-start(f32[512]{0:T(512)} %copy-done.11) | copy-start | bytes 6148
  103.4 62.1 %copy-start.4 = (f32[8,8,8]{2,1,0:T(8,128)S(1)}, f32[8,8,8]{2,1,0:T(8,128)}, u32[]{:S(2)}) copy-start(f32[8,8,8]{2,1,0:T(8,128)} %copy-done.3) | copy-start | bytes 6148
  103.4 58.9 %collective-permute-start.12 = (bf16[8,1,768]{2,1,0:T(2,128)(2,1)S(1)}, bf16[8,1,768]{2,1,0:T(2,128)(2,1)S(1)}, u32[]{:S(2)}, u32[]{:S(2)}) collective-permute-start(bf16[8,1,768]{2,1,0:T(2,128)(2,1)S(1)} %get-tuple-element.25), channel_id=1, source_target_pairs={{0,4},{4,8},{8,12},{12,16},{16,20},{20,24},{24,28},{1,5},{5,9},{9,... | collective-permute-start | bytes 36872 | tf_op jit(solution)/shard_map/ppermute | solution.py:17
  106.6 55.7 %collective-permute-start.13 = (bf16[8,1,768]{2,1,0:T(2,128)(2,1)S(1)}, bf16[8,1,768]{2,1,0:T(2,128)(2,1)S(1)}, u32[]{:S(2)}, u32[]{:S(2)}) collective-permute-start(bf16[8,1,768]{2,1,0:T(2,128)(2,1)S(1)} %get-tuple-element.26), channel_id=1, source_target_pairs={{4,0},{8,4},{12,8},{16,12},{20,16},{24,20},{28,24},{5,1},{9,5},{13... | collective-permute-start | bytes 36872 | tf_op jit(solution)/shard_map/ppermute | solution.py:19
  162.3 5.5 %collective-permute-start.14 = (bf16[1,10,768]{2,1,0:T(8,128)(2,1)S(1)}, bf16[1,10,768]{2,1,0:T(8,128)(2,1)S(1)}, u32[]{:S(2)}, u32[]{:S(2)}) collective-permute-start(bf16[1,10,768]{2,1,0:T(8,128)(2,1)S(1)} %get-tuple-element.17), channel_id=1, source_target_pairs={{0,1},{1,2},{2,3},{4,5},{5,6},{6,7},{8,9},{9,10},{10,11},{12,13},{... | collective-permute-start | bytes 46088 | tf_op jit(solution)/shard_map/ppermute | solution.py:17
  163.9 4.0 %collective-permute-start.15 = (bf16[1,10,768]{2,1,0:T(8,128)(2,1)S(1)}, bf16[1,10,768]{2,1,0:T(8,128)(2,1)S(1)}, u32[]{:S(2)}, u32[]{:S(2)}) collective-permute-start(bf16[1,10,768]{2,1,0:T(8,128)(2,1)S(1)} %get-tuple-element.18), channel_id=1, source_target_pairs={{1,0},{2,1},{3,2},{5,4},{6,5},{7,6},{9,8},{10,9},{11,10},{13,12},{... | collective-permute-start | bytes 46088 | tf_op jit(solution)/shard_map/ppermute | solution.py:19
  165.5 2.9 copy-start.6
  175.9 23.3 %all-to-all-start.2 = ((f32[8,64,96]{2,1,0:T(8,128)}), f32[8,64,96]{2,1,0:T(8,128)S(1)}, u32[]{:S(2)}, u32[]{:S(2)}) async-start(f32[8,64,96]{2,1,0:T(8,128)} %broadcast_divide_fusion), calls=%async_computation.2 | async-start | bytes 524288 | tf_op jit(solution)/shard_map/all_to_all | solution.py:146
  184.8 14.5 %copy-start.13 = (f32[8,96]{1,0:T(8,128)S(1)}, f32[8,96]{1,0:T(8,128)}, u32[]{:S(2)}) copy-start(f32[8,96]{1,0:T(8,128)} %param.17) | copy-start | bytes 9220
  184.8 14.5 %copy-start.14 = (f32[512,96]{0,1:T(8,128)S(1)}, f32[512,96]{0,1:T(8,128)}, u32[]{:S(2)}) copy-start(f32[512,96]{0,1:T(8,128)} %get-tuple-element.38) | copy-start | bytes 589828
  280.1 2.4 copy-start.1
Sparse Core Ops, SparseCore 0:
  102.6 59.6 all-reduce.11
  165.8 114.2 all-reduce.9
